TPU v7x, 32 devices: a whole 2x2x4 slice. The times are simulated.
32 devices in a mesh: fsdp: 4 (over z), tensor: 8 (over y, x, core).
Axes of the slice: x: 2, y: 2, z: 4, core: 2. Of those that a mesh axis runs over, the one named last changes fastest.
Arguments:
- tokens: bfloat16 [5120, 2048], P(('fsdp', 'tensor')), may hold values from -6 to 6
- gain_attn: bfloat16 [2048], replicated, may hold values from 0.099609375 to 1.8984375
- gain_mlp: bfloat16 [2048], replicated, may hold values from 0.099609375 to 1.8984375
- w_query: bfloat16 [2048, 2048], P('fsdp', 'tensor'), may hold values from -0.125 to 0.125
- w_key: bfloat16 [2048, 2048], P('fsdp', 'tensor'), may hold values from -0.125 to 0.125
- w_value: bfloat16 [2048, 2048], P('fsdp', 'tensor'), may hold values from -0.125 to 0.125
- w_out: bfloat16 [2048, 2048], P('tensor', 'fsdp'), may hold values from -0.5 to 0.5
- w_gate: bfloat16 [2048, 8192], P('fsdp', 'tensor'), may hold values from -0.125 to 0.125
- w_up: bfloat16 [2048, 8192], P('fsdp', 'tensor'), may hold values from -0.125 to 0.125
- w_down: bfloat16 [8192, 2048], P('tensor', 'fsdp'), may hold values from -0.09375 to 0.09375
- segment_ids: int32 [4, 1280], P('fsdp'), may hold values from 0 to 3, never falling along the last dimension, each value on 1 to 512 neighbouring positions
- out_grad: bfloat16 [5120, 2048], P(('fsdp', 'tensor')), may hold values from -6 to 6
Outputs:
- output: bfloat16 [5120, 2048], P(('fsdp', 'tensor'))
- tokens_grad: bfloat16 [5120, 2048], P(('fsdp', 'tensor'))
- gain_attn_grad: float32 [2048], replicated
- gain_mlp_grad: float32 [2048], replicated
- w_query_grad: float32 [2048, 2048], P('fsdp', 'tensor')
- w_key_grad: float32 [2048, 2048], P('fsdp', 'tensor')
- w_value_grad: float32 [2048, 2048], P('fsdp', 'tensor')
- w_out_grad: float32 [2048, 2048], P('tensor', 'fsdp')
- w_gate_grad: float32 [2048, 8192], P('fsdp', 'tensor')
- w_up_grad: float32 [2048, 8192], P('fsdp', 'tensor')
- w_down_grad: float32 [8192, 2048], P('tensor', 'fsdp')
Inputs may be any that keep to these rules, and one draw needn't show every extreme that they name: `segment_ids`: in each packed row the ids never fall; each sample has 1 to 512 tokens, and some sample in each row has exactly 512.
All inputs are finite; a program needn't handle non-finite values.
Results may differ from a plain program's by a relative error of at most 0.019.
Values may be sent and summed in bfloat16 or wider, within the bound.
A program may use at most 192 MiB of HBM per device.

v0:
```python
import math
import jax
import jax.numpy as jnp
from jax import lax
from jax.sharding import PartitionSpec as P

HEAD = 64
eps = 1e-05
rope_base = 130000.0


def dot_nt(left, right):
    return lax.dot_general(
        left, right, (((1,), (1,)), ((), ())), preferred_element_type=jnp.float32
    )


def dot_tn(left, right):
    return lax.dot_general(
        left, right, (((0,), (0,)), ((), ())), preferred_element_type=jnp.float32
    )


def rope_tables(segments):
    length = segments.shape[1]
    index = jnp.arange(length, dtype=jnp.int32)[None, :]
    change = jnp.concatenate(
        [jnp.ones((segments.shape[0], 1), dtype=bool), segments[:, 1:] != segments[:, :-1]], axis=1
    )
    start = lax.cummax(jnp.where(change, index, 0), axis=1)
    position = (index - start).astype(jnp.float32)
    half = jnp.arange(HEAD // 2, dtype=jnp.float32)
    inverse = jnp.exp(half * (-2.0 / HEAD) * math.log(rope_base))
    angle = position[:, :, None, None] * inverse[None, None, None, :]
    return (jnp.cos(angle), jnp.sin(angle))


def rotate(value, cosine, sine):
    half = value.shape[-1] // 2
    first = value[..., :half]
    second = value[..., half:]
    return jnp.concatenate(
        [first * cosine - second * sine, second * cosine + first * sine], axis=-1
    )


def norm_forward(value, gain):
    scale = lax.rsqrt(jnp.mean(value * value, axis=-1, keepdims=True) + eps)
    return (value * scale * gain, scale)


def norm_backward(value, scale, gain, grad):
    scaled_grad = grad * gain
    inner = jnp.mean(value * scaled_grad, axis=-1, keepdims=True)
    back = scale * scaled_grad - value * scale * scale * scale * inner
    gain_grad = jnp.sum(grad * value * scale, axis=0)
    return (back, gain_grad)


def row_mask(segments):
    length = segments.shape[0]
    index = jnp.arange(length, dtype=jnp.int32)
    return (segments[:, None] == segments[None, :]) & (index[None, :] <= index[:, None])


def row_scores(query, key, segments):
    scores = jnp.einsum("qhd,khd->hqk", query, key, preferred_element_type=jnp.float32) * HEAD ** (
        -0.5
    )
    return jnp.where(row_mask(segments)[None, :, :], scores, -1000000000.0)


def attend_row(inputs):
    query, key, value, segments = inputs
    scores = row_scores(query, key, segments)
    top = jnp.max(scores, axis=-1, keepdims=True)
    expo = jnp.exp(scores - top)
    total = jnp.sum(expo, axis=-1, keepdims=True)
    weights = (expo / total).astype(jnp.bfloat16)
    attended = jnp.einsum("hqk,khd->qhd", weights, value, preferred_element_type=jnp.float32)
    return (attended, (top + jnp.log(total))[..., 0])


def attend_back(inputs):
    query, key, value, segments, logsum, grad_out = inputs
    scores = row_scores(query, key, segments)
    weights = jnp.exp(scores - logsum[..., None])
    grad_value = jnp.einsum(
        "hqk,qhd->khd", weights.astype(jnp.bfloat16), grad_out, preferred_element_type=jnp.float32
    )
    grad_weights = jnp.einsum("qhd,khd->hqk", grad_out, value, preferred_element_type=jnp.float32)
    inner = jnp.sum(weights * grad_weights, axis=-1, keepdims=True)
    grad_scores = (weights * (grad_weights - inner)).astype(jnp.bfloat16)
    grad_query = jnp.einsum(
        "hqk,khd->qhd", grad_scores, key, preferred_element_type=jnp.float32
    ) * HEAD ** (-0.5)
    grad_key = jnp.einsum(
        "hqk,qhd->khd", grad_scores, query, preferred_element_type=jnp.float32
    ) * HEAD ** (-0.5)
    return (grad_query, grad_key, grad_value)


def shards(
    tokens,
    gain_attn,
    gain_mlp,
    w_query,
    w_key,
    w_value,
    w_out,
    w_gate,
    w_up,
    w_down,
    segment_ids,
    out_grad,
):
    rows_grp = segment_ids.shape[0]
    row_len = segment_ids.shape[1]
    local = (w_query, w_key, w_value, w_out, w_gate, w_up, w_down)
    gathered = (
        lax.all_gather(local[0], "fsdp", axis=0, tiled=True),
        lax.all_gather(local[1], "fsdp", axis=0, tiled=True),
        lax.all_gather(local[2], "fsdp", axis=0, tiled=True),
        lax.all_gather(local[3], "fsdp", axis=1, tiled=True),
        lax.all_gather(local[4], "fsdp", axis=0, tiled=True),
        lax.all_gather(local[5], "fsdp", axis=0, tiled=True),
        lax.all_gather(local[6], "fsdp", axis=1, tiled=True),
    )
    wq, wk, wv, wo, wg, wu, wd = gathered
    heads_dev = wq.shape[1] // HEAD
    group = rows_grp * row_len
    gain_a = gain_attn.astype(jnp.float32)
    gain_m = gain_mlp.astype(jnp.float32)
    cosine, sine = rope_tables(segment_ids)

    def heads(value):
        return value.reshape(rows_grp, row_len, heads_dev, HEAD)

    x = tokens.astype(jnp.float32)
    normed_local, scale_a = norm_forward(x, gain_a)
    normed_a = lax.all_gather(normed_local.astype(jnp.bfloat16), "tensor", axis=0, tiled=True)
    query = rotate(
        heads(jnp.dot(normed_a, wq, preferred_element_type=jnp.float32)), cosine, sine
    ).astype(jnp.bfloat16)
    key = rotate(
        heads(jnp.dot(normed_a, wk, preferred_element_type=jnp.float32)), cosine, sine
    ).astype(jnp.bfloat16)
    value = heads(jnp.dot(normed_a, wv, preferred_element_type=jnp.float32).astype(jnp.bfloat16))
    attended, logsum = lax.map(attend_row, (query, key, value, segment_ids))
    attended = attended.reshape(group, heads_dev * HEAD).astype(jnp.bfloat16)
    hidden = x + lax.psum_scatter(
        jnp.dot(attended, wo, preferred_element_type=jnp.float32),
        "tensor",
        scatter_dimension=0,
        tiled=True,
    )
    normed_hidden, scale_m = norm_forward(hidden, gain_m)
    normed_m = lax.all_gather(normed_hidden.astype(jnp.bfloat16), "tensor", axis=0, tiled=True)
    gate = jnp.dot(normed_m, wg, preferred_element_type=jnp.float32)
    up = jnp.dot(normed_m, wu, preferred_element_type=jnp.float32)
    sigma = jax.nn.sigmoid(gate)
    silu_gate = gate * sigma
    act = (silu_gate * up).astype(jnp.bfloat16)
    output = hidden + lax.psum_scatter(
        jnp.dot(act, wd, preferred_element_type=jnp.float32).astype(jnp.bfloat16),
        "tensor",
        scatter_dimension=0,
        tiled=True,
    ).astype(jnp.float32)
    wq, wk, wv, wo, wg, wu, wd = (
        lax.all_gather(local[0], "fsdp", axis=0, tiled=True),
        lax.all_gather(local[1], "fsdp", axis=0, tiled=True),
        lax.all_gather(local[2], "fsdp", axis=0, tiled=True),
        lax.all_gather(local[3], "fsdp", axis=1, tiled=True),
        lax.all_gather(local[4], "fsdp", axis=0, tiled=True),
        lax.all_gather(local[5], "fsdp", axis=0, tiled=True),
        lax.all_gather(local[6], "fsdp", axis=1, tiled=True),
    )
    grad_all = lax.all_gather(out_grad, "tensor", axis=0, tiled=True)
    grad_down = dot_tn(act, grad_all)
    grad_act = dot_nt(grad_all, wd)
    grad_gate = (grad_act * up * (sigma * (1.0 + gate * (1.0 - sigma)))).astype(jnp.bfloat16)
    grad_up = (grad_act * silu_gate).astype(jnp.bfloat16)
    grad_wgate = dot_tn(normed_m, grad_gate)
    grad_wup = dot_tn(normed_m, grad_up)
    grad_nm = lax.psum_scatter(
        dot_nt(grad_gate, wg) + dot_nt(grad_up, wu), "tensor", scatter_dimension=0, tiled=True
    )
    back_m, gain_m_part = norm_backward(hidden, scale_m, gain_m, grad_nm)
    grad_hidden = out_grad.astype(jnp.float32) + back_m
    grad_hidden_low = grad_hidden.astype(jnp.bfloat16)
    branch_all = lax.all_gather(grad_hidden_low, "tensor", axis=0, tiled=True)
    grad_wout = dot_tn(attended, branch_all)
    grad_attended = heads(dot_nt(branch_all, wo).astype(jnp.bfloat16))
    grad_query, grad_key, grad_value = lax.map(
        attend_back, (query, key, value, segment_ids, logsum, grad_attended)
    )
    grad_qpre = (
        rotate(grad_query, cosine, -sine).reshape(group, heads_dev * HEAD).astype(jnp.bfloat16)
    )
    grad_kpre = (
        rotate(grad_key, cosine, -sine).reshape(group, heads_dev * HEAD).astype(jnp.bfloat16)
    )
    grad_vpre = grad_value.reshape(group, heads_dev * HEAD).astype(jnp.bfloat16)
    grad_wq = dot_tn(normed_a, grad_qpre)
    grad_wk = dot_tn(normed_a, grad_kpre)
    grad_wv = dot_tn(normed_a, grad_vpre)
    grad_na_part = dot_nt(grad_qpre, wq) + dot_nt(grad_kpre, wk) + dot_nt(grad_vpre, wv)
    grad_na = lax.psum_scatter(
        grad_na_part.astype(jnp.bfloat16), "tensor", scatter_dimension=0, tiled=True
    ).astype(jnp.float32)
    back_a, gain_a_part = norm_backward(x, scale_a, gain_a, grad_na)
    tokens_grad = (grad_hidden + back_a).astype(jnp.bfloat16)
    gain_a_grad, gain_m_grad = lax.psum((gain_a_part, gain_m_part), ("fsdp", "tensor"))
    weight_grads = (
        lax.psum_scatter(
            grad_wq.astype(jnp.bfloat16), "fsdp", scatter_dimension=0, tiled=True
        ).astype(jnp.float32),
        lax.psum_scatter(
            grad_wk.astype(jnp.bfloat16), "fsdp", scatter_dimension=0, tiled=True
        ).astype(jnp.float32),
        lax.psum_scatter(
            grad_wv.astype(jnp.bfloat16), "fsdp", scatter_dimension=0, tiled=True
        ).astype(jnp.float32),
        lax.psum_scatter(
            grad_wout.astype(jnp.bfloat16), "fsdp", scatter_dimension=1, tiled=True
        ).astype(jnp.float32),
        lax.psum_scatter(
            grad_wgate.astype(jnp.bfloat16), "fsdp", scatter_dimension=0, tiled=True
        ).astype(jnp.float32),
        lax.psum_scatter(
            grad_wup.astype(jnp.bfloat16), "fsdp", scatter_dimension=0, tiled=True
        ).astype(jnp.float32),
        lax.psum_scatter(
            grad_down.astype(jnp.bfloat16), "fsdp", scatter_dimension=1, tiled=True
        ).astype(jnp.float32),
    )
    return (
        output.astype(jnp.bfloat16),
        tokens_grad,
        gain_a_grad,
        gain_m_grad,
        weight_grads[0],
        weight_grads[1],
        weight_grads[2],
        weight_grads[3],
        weight_grads[4],
        weight_grads[5],
        weight_grads[6],
    )


def solution(mesh):
    return jax.shard_map(
        shards,
        mesh=mesh,
        in_specs=(
            P(("fsdp", "tensor"), None),
            P(),
            P(),
            P("fsdp", "tensor"),
            P("fsdp", "tensor"),
            P("fsdp", "tensor"),
            P("tensor", "fsdp"),
            P("fsdp", "tensor"),
            P("fsdp", "tensor"),
            P("tensor", "fsdp"),
            P("fsdp", None),
            P(("fsdp", "tensor"), None),
        ),
        out_specs=(
            P(("fsdp", "tensor"), None),
            P(("fsdp", "tensor"), None),
            P(),
            P(),
            P("fsdp", "tensor"),
            P("fsdp", "tensor"),
            P("fsdp", "tensor"),
            P("tensor", "fsdp"),
            P("fsdp", "tensor"),
            P("fsdp", "tensor"),
            P("tensor", "fsdp"),
        ),
        check_vma=False,
    )
```

profile of v0, /device:TPU:0, one launch (start us, length us, event | category | flops | bytes accessed | tf_op | source)
XLA Modules:
  0.0 1231.1 jit_solution(9686080261791631921)
XLA Ops:
  10.5 2.1 fusion.18
  17.1 1.8 fusion.7
  20.3 20.0 %all-gather.18.cloned.1.call-done = bf16[2048,256]{1,0:T(8,128)(2,1)} async-done(((bf16[512,256]{1,0:T(8,128)(2,1)}), bf16[2048,256]{1,0:T(8,128)(2,1)}) %all-gather.18.cloned.1.call-update) | async-done | bytes 1048592 | tf_op jit(solution)/shard_map/all_gather | solution.py:122
  40.3 43.0 %all-gather.12.cloned.1.call-done = bf16[1280,2048]{1,0:T(8,128)(2,1)} async-done(((bf16[160,2048]{1,0:T(8,128)(2,1)}), bf16[1280,2048]{1,0:T(8,128)(2,1)}) %all-gather.12.cloned.1.call-update) | async-done | bytes 5242896 | tf_op jit(solution)/shard_map/all_gather | solution.py:141
  83.3 4.3 fusion.41
  87.7 25.2 %all-gather.16.cloned.1.call-done = bf16[2048,256]{1,0:T(8,128)(2,1)} async-done(((bf16[512,256]{1,0:T(8,128)(2,1)}), bf16[2048,256]{1,0:T(8,128)(2,1)}) %all-gather.16.cloned.1.call-update) | async-done | bytes 1048592 | tf_op jit(solution)/shard_map/all_gather | solution.py:121
  112.9 4.3 fusion.40
  117.6 11.1 fusion.39
  128.8 10.6 fusion.1
  139.4 2.4 all-gather.14.cloned.1.call-done
  141.8 4.3 convolution_convert_fusion.9
  146.1 21.8 %fusion.14 = bf16[4,64,1280]{2,1,0:T(8,128)(2,1)S(1)} fusion(bf16[1280,4,64]{0,2,1:T(8,128)(2,1)S(1)} %bitcast.97, f32[4,1280,1280]{1,2,0:T(8,128)} %get-tuple-element.91, f32[4,1280]{1,0:T(4,128)S(1)} %fusion.1, f32[4,1280]{1,0:T(4,128)S(1)} %get-tuple-element.90), kind=kOutput, calls=%fused_computation.41 | convolution fusion | flops 858849280 | bytes 27566080 | tf_op jit(solution)/shard_map/while/body/eval_jaxpr/hqk,khd->qhd/dot_general | solution.py:80
  167.9 2.8 all-gather.20.cloned.1.call-done
  170.6 6.7 fusion.42
  178.2 80.4 %reduce-scatter.12.cloned.1.call-done = f32[160,2048]{1,0:T(8,128)} async-done(((f32[1280,2048]{1,0:T(8,128)}), f32[160,2048]{1,0:T(8,128)}) %reduce-scatter.12.cloned.1.call-update) | async-done | bytes 1310736 | tf_op jit(solution)/shard_map/reduce_scatter | solution.py:151
  258.6 1.6 multiply_reduce_fusion.3
  263.3 77.6 %all-gather.26.cloned.1.call-done = bf16[2048,1024]{1,0:T(8,128)(2,1)} async-done(((bf16[512,1024]{1,0:T(8,128)(2,1)}), bf16[2048,1024]{1,0:T(8,128)(2,1)}) %all-gather.26.cloned.1.call-update) | async-done | bytes 4194320 | tf_op jit(solution)/shard_map/all_gather | solution.py:126
  340.9 42.1 %all-gather.22.cloned.1.call-done = bf16[1280,2048]{1,0:T(8,128)(2,1)} async-done(((bf16[160,2048]{1,0:T(8,128)(2,1)}), bf16[1280,2048]{1,0:T(8,128)(2,1)}) %all-gather.22.cloned.1.call-update) | async-done | bytes 5242896 | tf_op jit(solution)/shard_map/all_gather | solution.py:158
  383.0 10.2 fusion.44
  393.3 72.2 %all-gather.24.cloned.1.call-done = bf16[2048,1024]{1,0:T(8,128)(2,1)} async-done(((bf16[512,1024]{1,0:T(8,128)(2,1)}), bf16[2048,1024]{1,0:T(8,128)(2,1)}) %all-gather.24.cloned.1.call-update) | async-done | bytes 4194320 | tf_op jit(solution)/shard_map/all_gather | solution.py:125
  465.4 10.2 fusion.43
  475.6 70.5 %all-gather.28.cloned.1.call-done = bf16[1024,2048]{1,0:T(8,128)(2,1)} async-done(((bf16[1024,512]{1,0:T(8,128)(2,1)}), bf16[1024,2048]{1,0:T(8,128)(2,1)}) %all-gather.28.cloned.1.call-update) | async-done | bytes 4194320 | tf_op jit(solution)/shard_map/all_gather | solution.py:127
  546.2 41.6 %all-gather.30.cloned.1.call-done = bf16[1280,2048]{1,0:T(8,128)(2,1)} async-done(((bf16[160,2048]{1,0:T(8,128)(2,1)}), bf16[1280,2048]{1,0:T(8,128)(2,1)}) %all-gather.30.cloned.1.call-update) | async-done | bytes 5242896 | tf_op jit(solution)/shard_map/all_gather | solution.py:179
  587.7 14.7 %multiply_convert_fusion.1 = (bf16[1280,1024]{1,0:T(8,128)(2,1)S(1)}, bf16[1280,1024]{1,0:T(8,128)(2,1)S(1)}, bf16[1280,1024]{1,0:T(8,128)(2,1)}) fusion(f32[1280,1024]{1,0:T(8,128)} %fusion.43, f32[1280,1024]{1,0:T(8,128)} %fusion.44, bf16[1280,2048]{1,0:T(8,128)(2,1)} %all-gather.30.cloned.1.call-done, bf16[1024,2048]{1,0:T(8,128)(2,1)} %all-gather.28.cloned.1.call-done), kind=kOutput, calls=%fused_computation.17 | convolution fusion | flops 5388369920 | bytes 27787264 | tf_op jit(solution)/shard_map/dot_general | solution.py:13
  602.4 8.2 fusion.45
  610.7 11.0 convolution_add_fusion
  621.7 81.7 %reduce-scatter.16.cloned.1.call-done = f32[160,2048]{1,0:T(8,128)} async-done(((f32[1280,2048]{1,0:T(8,128)}), f32[160,2048]{1,0:T(8,128)}) %reduce-scatter.16.cloned.1.call-update) | async-done | bytes 1310736 | tf_op jit(solution)/shard_map/reduce_scatter | solution.py:186
  703.4 1.7 multiply_reduce_fusion.1
  705.1 2.6 fusion.38
  707.8 10.1 convolution_convert_fusion.1
  718.0 10.2 convolution_convert_fusion.2
  728.2 10.2 convolution_convert_fusion.3
  738.9 10.1 all-gather.32.cloned.1.call-done
  749.0 5.0 convolution_convert_fusion.4
  754.1 4.3 convolution_convert_fusion.8
  758.4 10.8 fusion.11
  769.2 5.1 convolution_convert_fusion.5
  774.3 16.7 %multiply_reduce_fusion = (f32[4,1280]{1,0:T(4,128)S(1)}, f32[4,1280,1280]{1,2,0:T(8,128)}) fusion(f32[4,1280,1280]{1,2,0:T(8,128)} %get-tuple-element.91, f32[4,1280]{1,0:T(4,128)S(1)} %log_add_fusion, bf16[1280,4,64]{0,2,1:T(8,128)(2,1)S(1)} %bitcast.90, bf16[1280,4,64]{0,2,1:T(8,128)(2,1)S(1)} %bitcast.98), kind=kOutput, calls=%fused_computation.3 | convolution fusion | flops 858516480 | bytes 53780480 | tf_op jit(solution)/shard_map/while/body/eval_jaxpr/qhd,khd->hqk/dot_general | solution.py:91
  791.2 22.5 %multiply_convert_fusion = bf16[4,1280,1280]{1,2,0:T(8,128)(2,1)} fusion(f32[4,1280,1280]{1,2,0:T(8,128)} %get-tuple-element.93, f32[4,1280,1280]{1,2,0:T(8,128)} %get-tuple-element.91, f32[4,1280]{1,0:T(4,128)S(1)} %get-tuple-element.92, f32[4,1280]{1,0:T(4,128)S(1)} %log_add_fusion), kind=kLoop, calls=%fused_computation.2 | loop fusion | flops 26214400 | bytes 65576960 | tf_op jit(solution)/shard_map/while/body/eval_jaxpr/convert_element_type | solution.py:93
  813.7 9.0 fusion.10
  822.8 7.2 fusion.9
  830.5 2.6 convolution_convert_fusion.6
  833.2 5.1 convolution_convert_fusion.7
  838.6 2.9 fusion.46
  841.5 5.6 fusion.47
  847.1 8.4 add_convert_fusion
  855.6 10.0 convolution_convert_fusion
  865.7 2.9 convert_element_type.194
  868.5 39.0 %reduce-scatter.30.cloned.1.call-done = bf16[512,1024]{1,0:T(8,128)(2,1)} async-done(((bf16[2048,1024]{1,0:T(8,128)(2,1)}), bf16[512,1024]{1,0:T(8,128)(2,1)}) %reduce-scatter.30.cloned.1.call-update) | async-done | bytes 1048592 | tf_op jit(solution)/shard_map/reduce_scatter | solution.py:231
  907.5 2.8 convert_element_type.192
  910.3 76.6 %reduce-scatter.28.cloned.1.call-done = bf16[512,1024]{1,0:T(8,128)(2,1)} async-done(((bf16[2048,1024]{1,0:T(8,128)(2,1)}), bf16[512,1024]{1,0:T(8,128)(2,1)}) %reduce-scatter.28.cloned.1.call-update) | async-done | bytes 1048592 | tf_op jit(solution)/shard_map/reduce_scatter | solution.py:228
  986.9 2.8 convert_element_type.190
  989.7 27.2 %reduce-scatter.26.cloned.1.call-done = bf16[256,512]{1,0:T(8,128)(2,1)} async-done(((bf16[256,2048]{1,0:T(8,128)(2,1)}), bf16[256,512]{1,0:T(8,128)(2,1)}) %reduce-scatter.26.cloned.1.call-update) | async-done | bytes 262160 | tf_op jit(solution)/shard_map/reduce_scatter | solution.py:225
  1016.9 1.8 convert_element_type.188
  1018.7 26.1 %reduce-scatter.24.cloned.1.call-done = bf16[512,256]{1,0:T(8,128)(2,1)} async-done(((bf16[2048,256]{1,0:T(8,128)(2,1)}), bf16[512,256]{1,0:T(8,128)(2,1)}) %reduce-scatter.24.cloned.1.call-update) | async-done | bytes 262160 | tf_op jit(solution)/shard_map/reduce_scatter | solution.py:222
  1044.8 1.8 convert_element_type.186
  1046.6 26.5 %reduce-scatter.22.cloned.1.call-done = bf16[512,256]{1,0:T(8,128)(2,1)} async-done(((bf16[2048,256]{1,0:T(8,128)(2,1)}), bf16[512,256]{1,0:T(8,128)(2,1)}) %reduce-scatter.22.cloned.1.call-update) | async-done | bytes 262160 | tf_op jit(solution)/shard_map/reduce_scatter | solution.py:219
  1073.1 1.8 convert_element_type.184
  1074.9 26.2 %reduce-scatter.20.cloned.1.call-done = bf16[512,256]{1,0:T(8,128)(2,1)} async-done(((bf16[2048,256]{1,0:T(8,128)(2,1)}), bf16[512,256]{1,0:T(8,128)(2,1)}) %reduce-scatter.20.cloned.1.call-update) | async-done | bytes 262160 | tf_op jit(solution)/shard_map/reduce_scatter | solution.py:216
  1101.0 1.8 convert_element_type.182
  1102.8 57.3 %reduce-scatter.18.cloned.1.call-done = bf16[160,2048]{1,0:T(8,128)(2,1)} async-done(((bf16[1280,2048]{1,0:T(8,128)(2,1)}), bf16[160,2048]{1,0:T(8,128)(2,1)}) %reduce-scatter.18.cloned.1.call-update) | async-done | bytes 655376 | tf_op jit(solution)/shard_map/reduce_scatter | solution.py:209
  1161.6 39.8 %all-reduce = (f32[2048]{0:T(1024)}, f32[2048]{0:T(1024)}) all-reduce(f32[2048]{0:T(1024)S(1)} %get-tuple-element.54, f32[2048]{0:T(1024)S(1)} %get-tuple-element.52), channel_id=1, replica_groups=mesh['fsdp'=4,'tensor'=8] {'fsdp','tensor'}, use_global_device_ids=true, to_apply=%region_14.15 | all-reduce | flops 4096 | bytes 32768 | tf_op jit(solution)/shard_map/psum | solution.py:214
  1201.4 19.3 %reduce-scatter.14.cloned.1.call-done = bf16[160,2048]{1,0:T(8,128)(2,1)} async-done(((bf16[1280,2048]{1,0:T(8,128)(2,1)}), bf16[160,2048]{1,0:T(8,128)(2,1)}) %reduce-scatter.14.cloned.1.call-update) | async-done | bytes 655376 | tf_op jit(solution)/shard_map/reduce_scatter | solution.py:164
  1220.7 3.4 fusion.23
  (127 shorter events, 16.7 us)
Async XLA Ops:
  7.2 33.1 %all-gather.18.cloned.1.call-start = ((), (), s32[]{:S(2)}) async-start(), calls=%async_computation.14 | async-start | bytes 1310720 | tf_op jit(solution)/shard_map/all_gather | solution.py:122
  7.9 75.4 %all-gather.12.cloned.1.call-start = ((), (), s32[]{:S(2)}) async-start(), calls=%async_computation.11 | async-start | bytes 5898240 | tf_op jit(solution)/shard_map/all_gather | solution.py:141
  8.6 1.3 copy-start.17
  10.0 0.6 copy-start.19
  12.7 100.2 %all-gather.16.cloned.1.call-start = ((), (), s32[]{:S(2)}) async-start(), calls=%async_computation.13 | async-start | bytes 1310720 | tf_op jit(solution)/shard_map/all_gather | solution.py:121
  13.4 128.3 %all-gather.14.cloned.1.call-start = ((), (), s32[]{:S(2)}) async-start(), calls=%async_computation.12 | async-start | bytes 1310720 | tf_op jit(solution)/shard_map/all_gather | solution.py:123
  14.0 156.6 %all-gather.20.cloned.1.call-start = ((), (), s32[]{:S(2)}) async-start(), calls=%async_computation.15 | async-start | bytes 1310720 | tf_op jit(solution)/shard_map/all_gather | solution.py:124
  14.6 243.9 %reduce-scatter.12.cloned.1.call-start = ((), (), s32[]{:S(2)}) async-start(), calls=%async_computation.16 | async-start | bytes 11796480 | tf_op jit(solution)/shard_map/reduce_scatter | solution.py:151
  20.3 97.0 %copy-start.4 = (f32[1280,32]{0,1:T(8,128)}, f32[1280,32]{0,1:T(8,128)S(1)}, u32[]{:S(2)}) copy-start(f32[1280,32]{0,1:T(8,128)S(1)} %get-tuple-element.89) | copy-start | bytes 491524
  117.6 11.1 copy-start.6
  117.6 11.1 copy-start.8
  117.6 11.1 copy-start.10
  117.6 11.1 copy-start.12
  177.3 0.8 copy-start.21
  177.3 81.2 %copy-start = (bf16[160,2048]{1,0:T(8,128)(2,1)S(1)}, bf16[160,2048]{1,0:T(8,128)(2,1)}, u32[]{:S(2)}) copy-start(bf16[160,2048]{1,0:T(8,128)(2,1)} %param.12) | copy-start | bytes 1966084
  177.4 163.5 %all-gather.26.cloned.1.call-start = ((), (), s32[]{:S(2)}) async-start(), calls=%async_computation.19 | async-start | bytes 5242880 | tf_op jit(solution)/shard_map/all_gather | solution.py:126
  178.1 204.9 %all-gather.22.cloned.1.call-start = ((), (), s32[]{:S(2)}) async-start(), calls=%async_computation.17 | async-start | bytes 5898240 | tf_op jit(solution)/shard_map/all_gather | solution.py:158
  261.2 204.2 %all-gather.24.cloned.1.call-start = ((), (), s32[]{:S(2)}) async-start(), calls=%async_computation.18 | async-start | bytes 5242880 | tf_op jit(solution)/shard_map/all_gather | solution.py:125
  261.9 284.2 %all-gather.28.cloned.1.call-start = ((), (), s32[]{:S(2)}) async-start(), calls=%async_computation.20 | async-start | bytes 5242880 | tf_op jit(solution)/shard_map/all_gather | solution.py:127
  262.5 325.2 %all-gather.30.cloned.1.call-start = ((), (), s32[]{:S(2)}) async-start(), calls=%async_computation.22 | async-start | bytes 5898240 | tf_op jit(solution)/shard_map/all_gather | solution.py:179
  263.2 440.2 %reduce-scatter.16.cloned.1.call-start = ((), (), s32[]{:S(2)}) async-start(), calls=%async_computation.23 | async-start | bytes 11796480 | tf_op jit(solution)/shard_map/reduce_scatter | solution.py:186
  587.7 14.7 %copy-start.23 = (bf16[2048,1024]{1,0:T(8,128)(2,1)S(1)}, bf16[2048,1024]{1,0:T(8,128)(2,1)}, u32[]{:S(2)}) copy-start(bf16[2048,1024]{1,0:T(8,128)(2,1)} %all-gather.24.cloned.1.call-done) | copy-start | bytes 12582916
  602.4 8.3 copy-start.25
  602.4 8.3 copy-start.24
  602.4 8.3 copy-start.22
  621.7 83.4 %copy-start.3 = (bf16[160,2048]{1,0:T(8,128)(2,1)S(1)}, bf16[160,2048]{1,0:T(8,128)(2,1)}, u32[]{:S(2)}) copy-start(bf16[160,2048]{1,0:T(8,128)(2,1)} %param.23) | copy-start | bytes 1966084
  621.7 127.3 %all-gather.32.cloned.1.call-start = ((), (), s32[]{:S(2)}) async-start(), calls=%async_computation.24 | async-start | bytes 5898240 | tf_op jit(solution)/shard_map/all_gather | solution.py:192
  707.8 157.9 %reduce-scatter.32.cloned.1.call-start = ((), (), s32[]{:S(2)}) async-start(), calls=%async_computation.32 | async-start | bytes 5242880 | tf_op jit(solution)/shard_map/reduce_scatter | solution.py:234
  717.9 189.6 %reduce-scatter.30.cloned.1.call-start = ((), (), s32[]{:S(2)}) async-start(), calls=%async_computation.31 | async-start | bytes 5242880 | tf_op jit(solution)/shard_map/reduce_scatter | solution.py:231
  728.2 258.8 %reduce-scatter.28.cloned.1.call-start = ((), (), s32[]{:S(2)}) async-start(), calls=%async_computation.30 | async-start | bytes 5242880 | tf_op jit(solution)/shard_map/reduce_scatter | solution.py:228
  738.4 278.4 %reduce-scatter.26.cloned.1.call-start = ((), (), s32[]{:S(2)}) async-start(), calls=%async_computation.29 | async-start | bytes 1310720 | tf_op jit(solution)/shard_map/reduce_scatter | solution.py:225
  754.0 290.8 %reduce-scatter.24.cloned.1.call-start = ((), (), s32[]{:S(2)}) async-start(), calls=%async_computation.28 | async-start | bytes 1310720 | tf_op jit(solution)/shard_map/reduce_scatter | solution.py:222
  791.0 282.1 %reduce-scatter.22.cloned.1.call-start = ((), (), s32[]{:S(2)}) async-start(), calls=%async_computation.27 | async-start | bytes 1310720 | tf_op jit(solution)/shard_map/reduce_scatter | solution.py:219
  791.2 22.5 %copy-start.11 = (bf16[1280,4,32]{0,2,1:T(8,128)(2,1)S(1)}, bf16[1280,4,32]{0,2,1:T(8,128)(2,1)}, u32[]{:S(2)}) copy-start(bf16[1280,4,32]{0,2,1:T(8,128)(2,1)} %copy-done.10) | copy-start | bytes 983044
  791.2 22.5 %copy-start.13 = (bf16[1280,4,32]{0,2,1:T(8,128)(2,1)S(1)}, bf16[1280,4,32]{0,2,1:T(8,128)(2,1)}, u32[]{:S(2)}) copy-start(bf16[1280,4,32]{0,2,1:T(8,128)(2,1)} %copy-done.12) | copy-start | bytes 983044
  813.7 9.0 copy-start.7
  813.7 9.0 copy-start.9
  813.7 16.7 %slice-start = ((s8[5242880]{0:T(1024)(128)(4,1)}), s8[1048576]{0:T(1024)(128)(4,1)S(1)}, s32[]{:S(2)}) async-start(s8[5242880]{0:T(1024)(128)(4,1)} %bitcast.104), calls=%async_computation.33 | async-start | bytes 2097152
  822.7 7.3 copy-start.5
  822.7 7.3 copy-start.16
  822.8 7.7 slice-start.1
  833.1 267.9 %reduce-scatter.20.cloned.1.call-start = ((), (), s32[]{:S(2)}) async-start(), calls=%async_computation.26 | async-start | bytes 1310720 | tf_op jit(solution)/shard_map/reduce_scatter | solution.py:216
  838.3 321.8 %reduce-scatter.18.cloned.1.call-start = ((), (), s32[]{:S(2)}) async-start(), calls=%async_computation.25 | async-start | bytes 5898240 | tf_op jit(solution)/shard_map/reduce_scatter | solution.py:209
  838.5 2.9 copy-start.14
  841.5 5.6 copy-start.15
  855.5 365.1 %reduce-scatter.14.cloned.1.call-start = ((), (), s32[]{:S(2)}) async-start(), calls=%async_computation.21 | async-start | bytes 5898240 | tf_op jit(solution)/shard_map/reduce_scatter | solution.py:164
  868.5 291.6 %copy-start.1 = (bf16[160,2048]{1,0:T(8,128)(2,1)S(1)}, bf16[160,2048]{1,0:T(8,128)(2,1)}, u32[]{:S(2)}) copy-start(bf16[160,2048]{1,0:T(8,128)(2,1)} %param.12) | copy-start | bytes 1966084
  868.5 291.6 %copy-start.18 = (f32[2048]{0:T(1024)S(1)}, f32[2048]{0:T(1024)}, u32[]{:S(2)}) copy-start(f32[2048]{0:T(1024)} %copy-done.17) | copy-start | bytes 24580
  868.5 291.6 %copy-start.20 = (f32[160]{0:T(256)S(1)}, f32[160]{0:T(256)}, u32[]{:S(2)}) copy-start(f32[160]{0:T(256)} %copy-done.19) | copy-start | bytes 1924
  910.3 310.4 %copy-start.2 = (f32[160,2048]{1,0:T(8,128)S(1)}, f32[160,2048]{1,0:T(8,128)}, u32[]{:S(2)}) copy-start(f32[160,2048]{1,0:T(8,128)} %reduce-scatter.16.cloned.1.call-done) | copy-start | bytes 3932164
Sparse Core Ops, SparseCore 0:
  9.6 30.6 all-gather.17
  42.8 40.5 all-gather.11
  84.9 27.9 all-gather.15
  114.3 27.4 all-gather.13
  143.2 27.4 all-gather.19
  177.5 81.0 reduce-scatter.11
  260.1 80.7 all-gather.25
  343.4 39.6 all-gather.21
  384.6 80.7 all-gather.23
  466.8 79.2 all-gather.27
  548.0 39.6 all-gather.29
  621.8 81.5 reduce-scatter.15
  707.9 41.0 all-gather.31
  751.2 76.7 reduce-scatter.31
  830.2 77.2 reduce-scatter.29
  909.7 77.2 reduce-scatter.27
  989.2 27.6 reduce-scatter.25
  1019.0 25.7 reduce-scatter.23
  1047.2 25.8 reduce-scatter.21
  1075.2 25.7 reduce-scatter.19
  1104.8 55.2 reduce-scatter.17
  1163.5 57.1 reduce-scatter.13
where the time goes:
time: 1240 us; the launch traced here: 1230 us
  waiting for transfers between devices  873 us (70%)
  matrix products  230 us (19%)
  other arithmetic  70.7 us (6%)
  blocking collectives  39.8 us (3%)
  between operations  15 us (1%)
    reduce_scatter x1, waiting for transfers between devices, shards(): lax.psum_scatter(dot_nt(grad_gate, wg) + dot_nt(grad_up, wu), 'tensor', s...  81.7 us
    reduce_scatter x1, waiting for transfers between devices, shards(): lax.psum_scatter(jnp.dot(attended, wo, preferred_element_type=jnp.float32...  80.4 us
    all_gather x1, waiting for transfers between devices, shards(): lax.all_gather(local[5], 'fsdp', axis=0, tiled=True)  77.6 us
    reduce_scatter x1, waiting for transfers between devices, shards(): lax.psum_scatter(grad_wgate.astype(jnp.bfloat16), 'fsdp', scatter_dimensi...  76.6 us
    all_gather x1, waiting for transfers between devices, shards(): lax.all_gather(local[4], 'fsdp', axis=0, tiled=True)  72.2 us
    all_gather x1, waiting for transfers between devices, shards(): lax.all_gather(local[6], 'fsdp', axis=1, tiled=True)  70.5 us
    reduce_scatter x1, waiting for transfers between devices, shards(): lax.psum_scatter(grad_na_part.astype(jnp.bfloat16), 'tensor', scatter_dim...  57.3 us
    dot_general x7, matrix products, dot_nt(): lax.dot_general(left, right, (((1,), (1,)), ((), ())), preferred_element_...  55.2 us
  transfers between devices with their start and end apart: 22, of which 21 were waited for; matrix products, arithmetic and copies ran while one was open for 21% of the time, Pallas kernels for 0%

commit v1 on v0

--- a/solution.py
+++ b/solution.py
@@ -176,7 +176,13 @@
         lax.all_gather(local[5], "fsdp", axis=0, tiled=True),
         lax.all_gather(local[6], "fsdp", axis=1, tiled=True),
     )
-    grad_all = lax.all_gather(out_grad, "tensor", axis=0, tiled=True)
+    n_dev = lax.axis_size("tensor")
+    block, blocks = (out_grad, [out_grad])
+    for _ in range(n_dev - 1):
+        block = lax.ppermute(block, "tensor", [(i, (i + 1) % n_dev) for i in range(n_dev)])
+        blocks.insert(0, block)
+    merged = jnp.concatenate(blocks, axis=0)
+    grad_all = jnp.roll(merged, (lax.axis_index("tensor") + 1) * out_grad.shape[0], axis=0)
     grad_down = dot_tn(act, grad_all)
     grad_act = dot_nt(grad_all, wd)
     grad_gate = (grad_act * up * (sigma * (1.0 + gate * (1.0 - sigma)))).astype(jnp.bfloat16)

time: 1240 us -> 1200 us (0.968)
  waiting for transfers between devices: 873 us -> 805 us
  local copies, waits for them, and re-layouts: 0.97 us -> 25.6 us
    all_gather x1, waiting for transfers between devices: 77.6 us -> 0.01 us  [shards(): lax.all_gather(local[5], 'fsdp', axis=0, tiled=True)]
    ppermute x0 -> x7, waiting for transfers between devices: none -> 76.6 us  [shards(): lax.ppermute(block, 'tensor', [(i, (i + 1) % n_dev) for i in range(n_dev)])]
    all_gather x1 -> x0, waiting for transfers between devices: 41.6 us -> none  [shards(): grad_all = lax.all_gather(out_grad, 'tensor', axis=0, tiled=True)]
    unnamed x56 -> x93, local copies, waits for them, and re-layouts: 0.68 us -> 24.4 us
    all_gather x1, waiting for transfers between devices: 42.1 us -> 20.4 us  [shards(): lax.all_gather(normed_hidden.astype(jnp.bfloat16), 'tensor', axis=0, tile...]
  transfers between devices with their start and end apart: 22 -> 28, of which waited for: 21 -> 26; matrix products, arithmetic and copies ran while one was open for 21% -> 23% of each run, Pallas kernels for 0% -> 0%
where the time goes in v1:
time: 1200 us; the launch traced here: 1190 us
  waiting for transfers between devices  805 us (67%)
  matrix products  230 us (19%)
  other arithmetic  70.7 us (6%)
  blocking collectives  39.8 us (3%)
  local copies, waits for them, and re-layouts  25.6 us (2%)
  between operations  15.3 us (1%)
    reduce_scatter x1, waiting for transfers between devices, shards(): lax.psum_scatter(jnp.dot(attended, wo, preferred_element_type=jnp.float32...  80.4 us
    reduce_scatter x1, waiting for transfers between devices, shards(): lax.psum_scatter(dot_nt(grad_gate, wg) + dot_nt(grad_up, wu), 'tensor', s...  80.2 us
    reduce_scatter x1, waiting for transfers between devices, shards(): lax.psum_scatter(grad_wgate.astype(jnp.bfloat16), 'fsdp', scatter_dimensi...  76.7 us
    ppermute x7, waiting for transfers between devices, shards(): lax.ppermute(block, 'tensor', [(i, (i + 1) % n_dev) for i in range(n_dev)])  76.6 us
    all_gather x1, waiting for transfers between devices, shards(): lax.all_gather(local[4], 'fsdp', axis=0, tiled=True)  72.1 us
    all_gather x1, waiting for transfers between devices, shards(): lax.all_gather(local[6], 'fsdp', axis=1, tiled=True)  70.5 us
    reduce_scatter x1, waiting for transfers between devices, shards(): lax.psum_scatter(grad_na_part.astype(jnp.bfloat16), 'tensor', scatter_dim...  57.1 us
    dot_general x7, matrix products, dot_nt(): lax.dot_general(left, right, (((1,), (1,)), ((), ())), preferred_element_...  54.5 us
  transfers between devices with their start and end apart: 28, of which 26 were waited for; matrix products, arithmetic and copies ran while one was open for 23% of the time, Pallas kernels for 0%

profile of v1, /device:TPU:0, one launch (start us, length us, event | category | flops | bytes accessed | tf_op | source)
XLA Modules:
  0.0 1188.0 jit_solution(4787386813413187008)
XLA Ops:
  10.5 2.1 fusion.25
  20.3 20.0 %all-gather.17.cloned.1.call-done = bf16[2048,256]{1,0:T(8,128)(2,1)} async-done(((bf16[512,256]{1,0:T(8,128)(2,1)}), bf16[2048,256]{1,0:T(8,128)(2,1)}) %all-gather.17.cloned.1.call-update) | async-done | bytes 1048592 | tf_op jit(solution)/shard_map/all_gather | solution.py:122
  40.3 43.0 %all-gather.11.cloned.1.call-done = bf16[1280,2048]{1,0:T(8,128)(2,1)} async-done(((bf16[160,2048]{1,0:T(8,128)(2,1)}), bf16[1280,2048]{1,0:T(8,128)(2,1)}) %all-gather.11.cloned.1.call-update) | async-done | bytes 5242896 | tf_op jit(solution)/shard_map/all_gather | solution.py:141
  83.3 4.3 fusion.50
  87.7 25.2 %all-gather.15.cloned.1.call-done = bf16[2048,256]{1,0:T(8,128)(2,1)} async-done(((bf16[512,256]{1,0:T(8,128)(2,1)}), bf16[2048,256]{1,0:T(8,128)(2,1)}) %all-gather.15.cloned.1.call-update) | async-done | bytes 1048592 | tf_op jit(solution)/shard_map/all_gather | solution.py:121
  112.9 4.3 fusion.49
  117.6 11.1 fusion.48
  128.7 10.6 fusion.1
  139.3 2.4 all-gather.13.cloned.1.call-done
  141.8 4.3 convolution_convert_fusion.8
  147.0 22.7 %fusion.21 = bf16[4,64,1280]{2,1,0:T(8,128)(2,1)S(1)} fusion(bf16[1280,4,64]{0,2,1:T(8,128)(2,1)S(1)} %bitcast.95, f32[4,1280,1280]{1,2,0:T(8,128)} %get-tuple-element.91, f32[4,1280]{1,0:T(4,128)S(1)} %fusion.1, f32[4,1280]{1,0:T(4,128)S(1)} %get-tuple-element.90), kind=kOutput, calls=%fused_computation.45 | convolution fusion | flops 858849280 | bytes 27566080 | tf_op jit(solution)/shard_map/while/body/eval_jaxpr/hqk,khd->qhd/dot_general | solution.py:80
  170.6 6.7 fusion.51
  178.2 80.4 %reduce-scatter.12.cloned.1.call-done = f32[160,2048]{1,0:T(8,128)} async-done(((f32[1280,2048]{1,0:T(8,128)}), f32[160,2048]{1,0:T(8,128)}) %reduce-scatter.12.cloned.1.call-update) | async-done | bytes 1310736 | tf_op jit(solution)/shard_map/reduce_scatter | solution.py:151
  262.1 10.9 collective-permute-done
  273.0 10.9 collective-permute-done.1
  283.9 10.9 collective-permute-done.2
  295.6 10.9 collective-permute-done.3
  307.4 10.9 collective-permute-done.4
  319.1 11.0 collective-permute-done.5
  330.2 11.1 collective-permute-done.6
  345.4 2.0 constant_dynamic-update-slice_fusion.13
  347.4 2.1 constant_dynamic-update-slice_fusion.12
  355.2 2.0 constant_dynamic-update-slice_fusion.6
  362.7 20.4 %all-gather.21.cloned.1.call-done = bf16[1280,2048]{1,0:T(8,128)(2,1)} async-done(((bf16[160,2048]{1,0:T(8,128)(2,1)}), bf16[1280,2048]{1,0:T(8,128)(2,1)}) %all-gather.21.cloned.1.call-update) | async-done | bytes 5242896 | tf_op jit(solution)/shard_map/all_gather | solution.py:158
  383.1 10.3 fusion.53
  393.3 72.1 %all-gather.23.cloned.1.call-done = bf16[2048,1024]{1,0:T(8,128)(2,1)} async-done(((bf16[512,1024]{1,0:T(8,128)(2,1)}), bf16[2048,1024]{1,0:T(8,128)(2,1)}) %all-gather.23.cloned.1.call-update) | async-done | bytes 4194320 | tf_op jit(solution)/shard_map/all_gather | solution.py:125
  465.4 10.3 fusion.52
  475.7 70.5 %all-gather.27.cloned.1.call-done = bf16[1024,2048]{1,0:T(8,128)(2,1)} async-done(((bf16[1024,512]{1,0:T(8,128)(2,1)}), bf16[1024,2048]{1,0:T(8,128)(2,1)}) %all-gather.27.cloned.1.call-update) | async-done | bytes 4194320 | tf_op jit(solution)/shard_map/all_gather | solution.py:127
  546.2 14.0 %multiply_convert_fusion.1 = (bf16[1280,1024]{1,0:T(8,128)(2,1)S(1)}, bf16[1280,1024]{1,0:T(8,128)(2,1)S(1)}, bf16[1280,1024]{1,0:T(8,128)(2,1)}) fusion(f32[1280,1024]{1,0:T(8,128)} %fusion.52, f32[1280,1024]{1,0:T(8,128)} %fusion.53, bf16[1024,2048]{1,0:T(8,128)(2,1)} %all-gather.27.cloned.1.call-done, ...), kind=kOutput, calls=%fused_computation.17 | convolution fusion | flops 5388369920 | bytes 27787268 | tf_op jit(solution)/shard_map/dot_general | solution.py:13
  560.2 8.3 fusion.54
  568.6 11.3 convolution_add_fusion
  579.9 80.2 %reduce-scatter.16.cloned.1.call-done = f32[160,2048]{1,0:T(8,128)} async-done(((f32[1280,2048]{1,0:T(8,128)}), f32[160,2048]{1,0:T(8,128)}) %reduce-scatter.16.cloned.1.call-update) | async-done | bytes 1310736 | tf_op jit(solution)/shard_map/reduce_scatter | solution.py:192
  661.8 2.6 fusion.47
  664.5 9.9 fusion.13
  674.5 10.2 convolution_convert_fusion.1
  684.7 10.2 convolution_convert_fusion.2
  695.2 10.5 all-gather.29.cloned.1.call-done
  705.7 5.0 convolution_convert_fusion.3
  710.8 4.0 convolution_convert_fusion.7
  714.8 10.8 fusion.18
  725.6 5.1 convolution_convert_fusion.4
  730.7 16.7 %multiply_reduce_fusion = (f32[4,1280]{1,0:T(4,128)S(1)}, f32[4,1280,1280]{1,2,0:T(8,128)}) fusion(f32[4,1280,1280]{1,2,0:T(8,128)} %get-tuple-element.91, f32[4,1280]{1,0:T(4,128)S(1)} %log_add_fusion, bf16[1280,4,64]{0,2,1:T(8,128)(2,1)S(1)} %bitcast.88, bf16[1280,4,64]{0,2,1:T(8,128)(2,1)S(1)} %bitcast.96), kind=kOutput, calls=%fused_computation.3 | convolution fusion | flops 858516480 | bytes 53780480 | tf_op jit(solution)/shard_map/while/body/eval_jaxpr/qhd,khd->hqk/dot_general | solution.py:91
  747.7 22.4 %multiply_convert_fusion = bf16[4,1280,1280]{1,2,0:T(8,128)(2,1)} fusion(f32[4,1280,1280]{1,2,0:T(8,128)} %get-tuple-element.93, f32[4,1280,1280]{1,2,0:T(8,128)} %get-tuple-element.91, f32[4,1280]{1,0:T(4,128)S(1)} %get-tuple-element.92, f32[4,1280]{1,0:T(4,128)S(1)} %log_add_fusion), kind=kLoop, calls=%fused_computation.2 | loop fusion | flops 26214400 | bytes 65576960 | tf_op jit(solution)/shard_map/while/body/eval_jaxpr/convert_element_type | solution.py:93
  770.2 9.0 fusion.17
  779.2 7.2 fusion.16
  787.0 2.6 convolution_convert_fusion.5
  789.6 5.1 convolution_convert_fusion.6
  795.1 2.9 fusion.55
  798.0 5.6 fusion.56
  803.6 8.4 add_convert_fusion
  812.1 9.9 convolution_convert_fusion
  822.1 2.9 convert_element_type.194
  824.9 39.4 %reduce-scatter.30.cloned.1.call-done = bf16[512,1024]{1,0:T(8,128)(2,1)} async-done(((bf16[2048,1024]{1,0:T(8,128)(2,1)}), bf16[512,1024]{1,0:T(8,128)(2,1)}) %reduce-scatter.30.cloned.1.call-update) | async-done | bytes 1048592 | tf_op jit(solution)/shard_map/reduce_scatter | solution.py:237
  864.3 2.8 convert_element_type.192
  867.1 76.7 %reduce-scatter.28.cloned.1.call-done = bf16[512,1024]{1,0:T(8,128)(2,1)} async-done(((bf16[2048,1024]{1,0:T(8,128)(2,1)}), bf16[512,1024]{1,0:T(8,128)(2,1)}) %reduce-scatter.28.cloned.1.call-update) | async-done | bytes 1048592 | tf_op jit(solution)/shard_map/reduce_scatter | solution.py:234
  943.8 2.8 convert_element_type.190
  946.6 27.1 %reduce-scatter.26.cloned.1.call-done = bf16[256,512]{1,0:T(8,128)(2,1)} async-done(((bf16[256,2048]{1,0:T(8,128)(2,1)}), bf16[256,512]{1,0:T(8,128)(2,1)}) %reduce-scatter.26.cloned.1.call-update) | async-done | bytes 262160 | tf_op jit(solution)/shard_map/reduce_scatter | solution.py:231
  975.5 26.2 %reduce-scatter.24.cloned.1.call-done = bf16[512,256]{1,0:T(8,128)(2,1)} async-done(((bf16[2048,256]{1,0:T(8,128)(2,1)}), bf16[512,256]{1,0:T(8,128)(2,1)}) %reduce-scatter.24.cloned.1.call-update) | async-done | bytes 262160 | tf_op jit(solution)/shard_map/reduce_scatter | solution.py:228
  1003.4 26.3 %reduce-scatter.22.cloned.1.call-done = bf16[512,256]{1,0:T(8,128)(2,1)} async-done(((bf16[2048,256]{1,0:T(8,128)(2,1)}), bf16[512,256]{1,0:T(8,128)(2,1)}) %reduce-scatter.22.cloned.1.call-update) | async-done | bytes 262160 | tf_op jit(solution)/shard_map/reduce_scatter | solution.py:225
  1031.5 26.3 %reduce-scatter.20.cloned.1.call-done = bf16[512,256]{1,0:T(8,128)(2,1)} async-done(((bf16[2048,256]{1,0:T(8,128)(2,1)}), bf16[512,256]{1,0:T(8,128)(2,1)}) %reduce-scatter.20.cloned.1.call-update) | async-done | bytes 262160 | tf_op jit(solution)/shard_map/reduce_scatter | solution.py:222
  1059.6 57.1 %reduce-scatter.18.cloned.1.call-done = bf16[160,2048]{1,0:T(8,128)(2,1)} async-done(((bf16[1280,2048]{1,0:T(8,128)(2,1)}), bf16[160,2048]{1,0:T(8,128)(2,1)}) %reduce-scatter.18.cloned.1.call-update) | async-done | bytes 655376 | tf_op jit(solution)/shard_map/reduce_scatter | solution.py:215
  1118.3 39.8 %all-reduce = (f32[2048]{0:T(1024)}, f32[2048]{0:T(1024)}) all-reduce(f32[2048]{0:T(1024)S(1)} %get-tuple-element.54, f32[2048]{0:T(1024)S(1)} %get-tuple-element.52), channel_id=1, replica_groups=mesh['fsdp'=4,'tensor'=8] {'fsdp','tensor'}, use_global_device_ids=true, to_apply=%region_14.15 | all-reduce | flops 4096 | bytes 32768 | tf_op jit(solution)/shard_map/psum | solution.py:220
  1158.0 19.3 %reduce-scatter.14.cloned.1.call-done = bf16[160,2048]{1,0:T(8,128)(2,1)} async-done(((bf16[1280,2048]{1,0:T(8,128)(2,1)}), bf16[160,2048]{1,0:T(8,128)(2,1)}) %reduce-scatter.14.cloned.1.call-update) | async-done | bytes 655376 | tf_op jit(solution)/shard_map/reduce_scatter | solution.py:164
  1177.3 3.4 fusion.30
  (176 shorter events, 47.1 us)
Async XLA Ops:
  7.2 33.1 %all-gather.17.cloned.1.call-start = ((), (), s32[]{:S(2)}) async-start(), calls=%async_computation.14 | async-start | bytes 1310720 | tf_op jit(solution)/shard_map/all_gather | solution.py:122
  7.9 75.4 %all-gather.11.cloned.1.call-start = ((), (), s32[]{:S(2)}) async-start(), calls=%async_computation.11 | async-start | bytes 5898240 | tf_op jit(solution)/shard_map/all_gather | solution.py:141
  8.6 1.3 copy-start.28
  12.7 100.2 %all-gather.15.cloned.1.call-start = ((), (), s32[]{:S(2)}) async-start(), calls=%async_computation.13 | async-start | bytes 1310720 | tf_op jit(solution)/shard_map/all_gather | solution.py:121
  13.4 128.3 %all-gather.13.cloned.1.call-start = ((), (), s32[]{:S(2)}) async-start(), calls=%async_computation.12 | async-start | bytes 1310720 | tf_op jit(solution)/shard_map/all_gather | solution.py:123
  14.0 156.6 %all-gather.19.cloned.1.call-start = ((), (), s32[]{:S(2)}) async-start(), calls=%async_computation.15 | async-start | bytes 1310720 | tf_op jit(solution)/shard_map/all_gather | solution.py:124
  14.6 244.0 %reduce-scatter.12.cloned.1.call-start = ((), (), s32[]{:S(2)}) async-start(), calls=%async_computation.16 | async-start | bytes 11796480 | tf_op jit(solution)/shard_map/reduce_scatter | solution.py:151
  20.3 97.0 %copy-start.10 = (f32[1280,32]{0,1:T(8,128)}, f32[1280,32]{0,1:T(8,128)S(1)}, u32[]{:S(2)}) copy-start(f32[1280,32]{0,1:T(8,128)S(1)} %get-tuple-element.89) | copy-start | bytes 491524
  117.6 11.1 copy-start.14
  117.6 11.1 copy-start.16
  117.6 11.1 copy-start.18
  117.6 11.1 copy-start.20
  146.1 0.8 copy-start.12
  169.6 7.7 copy-start.25
  177.3 0.8 copy-start.32
  177.3 81.2 %copy-start = (bf16[160,2048]{1,0:T(8,128)(2,1)S(1)}, bf16[160,2048]{1,0:T(8,128)(2,1)}, u32[]{:S(2)}) copy-start(bf16[160,2048]{1,0:T(8,128)(2,1)} %param.12) | copy-start | bytes 1966084
  177.4 84.6 %copy-start.3 = (bf16[160,2048]{1,0:T(8,128)(2,1)S(1)}, bf16[160,2048]{1,0:T(8,128)(2,1)}, u32[]{:S(2)}) copy-start(bf16[160,2048]{1,0:T(8,128)(2,1)} %param.23) | copy-start | bytes 1966084
  177.4 185.3 %all-gather.25.cloned.1.call-start = ((), (), s32[]{:S(2)}) async-start(), calls=%async_computation.19 | async-start | bytes 5242880 | tf_op jit(solution)/shard_map/all_gather | solution.py:126
  178.1 204.9 %all-gather.21.cloned.1.call-start = ((), (), s32[]{:S(2)}) async-start(), calls=%async_computation.17 | async-start | bytes 5898240 | tf_op jit(solution)/shard_map/all_gather | solution.py:158
  261.2 204.2 %all-gather.23.cloned.1.call-start = ((), (), s32[]{:S(2)}) async-start(), calls=%async_computation.18 | async-start | bytes 5242880 | tf_op jit(solution)/shard_map/all_gather | solution.py:125
  261.9 284.2 %all-gather.27.cloned.1.call-start = ((), (), s32[]{:S(2)}) async-start(), calls=%async_computation.20 | async-start | bytes 5242880 | tf_op jit(solution)/shard_map/all_gather | solution.py:127
  262.0 11.0 collective-permute-start
  273.0 10.9 collective-permute-start.1
  283.9 10.9 collective-permute-start.2
  294.8 0.8 copy-start.4
  295.6 10.9 collective-permute-start.3
  307.4 10.9 collective-permute-start.4
  319.1 11.0 collective-permute-start.5
  330.1 11.2 collective-permute-start.6
  330.2 329.9 %reduce-scatter.16.cloned.1.call-start = ((), (), s32[]{:S(2)}) async-start(), calls=%async_computation.22 | async-start | bytes 11796480 | tf_op jit(solution)/shard_map/reduce_scatter | solution.py:192
  330.2 19.3 %copy-start.5 = (bf16[160,2048]{1,0:T(8,128)(2,1)S(1)}, bf16[160,2048]{1,0:T(8,128)(2,1)}, u32[]{:S(2)}) copy-start(bf16[160,2048]{1,0:T(8,128)(2,1)} %copy-done.4) | copy-start | bytes 1966084
  345.4 11.8 copy-start.9
  347.4 10.7 copy-start.7
  546.2 14.1 %copy-start.34 = (bf16[2048,1024]{1,0:T(8,128)(2,1)S(1)}, bf16[2048,1024]{1,0:T(8,128)(2,1)}, u32[]{:S(2)}) copy-start(bf16[2048,1024]{1,0:T(8,128)(2,1)} %all-gather.23.cloned.1.call-done) | copy-start | bytes 12582916
  560.2 8.3 copy-start.36
  560.2 8.3 copy-start.35
  560.2 8.3 copy-start.33
  579.8 125.8 %all-gather.29.cloned.1.call-start = ((), (), s32[]{:S(2)}) async-start(), calls=%async_computation.23 | async-start | bytes 5898240 | tf_op jit(solution)/shard_map/all_gather | solution.py:198
  664.4 157.6 %reduce-scatter.32.cloned.1.call-start = ((), (), s32[]{:S(2)}) async-start(), calls=%async_computation.31 | async-start | bytes 5242880 | tf_op jit(solution)/shard_map/reduce_scatter | solution.py:240
  674.4 189.9 %reduce-scatter.30.cloned.1.call-start = ((), (), s32[]{:S(2)}) async-start(), calls=%async_computation.30 | async-start | bytes 5242880 | tf_op jit(solution)/shard_map/reduce_scatter | solution.py:237
  684.7 21.0 %copy-start.26 = (bf16[4,64,1280]{2,1,0:T(8,128)(2,1)S(1)}, bf16[4,64,1280]{2,1,0:T(8,128)(2,1)}, u32[]{:S(2)}) copy-start(bf16[4,64,1280]{2,1,0:T(8,128)(2,1)} %copy-done.25) | copy-start | bytes 1966084
  684.7 259.1 %reduce-scatter.28.cloned.1.call-start = ((), (), s32[]{:S(2)}) async-start(), calls=%async_computation.29 | async-start | bytes 5242880 | tf_op jit(solution)/shard_map/reduce_scatter | solution.py:234
  695.0 278.7 %reduce-scatter.26.cloned.1.call-start = ((), (), s32[]{:S(2)}) async-start(), calls=%async_computation.28 | async-start | bytes 1310720 | tf_op jit(solution)/shard_map/reduce_scatter | solution.py:231
  695.2 15.5 %copy-start.23 = (bf16[256,2048]{1,0:T(8,128)(2,1)S(1)}, bf16[256,2048]{1,0:T(8,128)(2,1)}, u32[]{:S(2)}) copy-start(bf16[256,2048]{1,0:T(8,128)(2,1)} %all-gather.19.cloned.1.call-done) | copy-start | bytes 3145732
  710.7 291.0 %reduce-scatter.24.cloned.1.call-start = ((), (), s32[]{:S(2)}) async-start(), calls=%async_computation.27 | async-start | bytes 1310720 | tf_op jit(solution)/shard_map/reduce_scatter | solution.py:228
  725.6 5.1 copy-start.13
  747.5 282.3 %reduce-scatter.22.cloned.1.call-start = ((), (), s32[]{:S(2)}) async-start(), calls=%async_computation.26 | async-start | bytes 1310720 | tf_op jit(solution)/shard_map/reduce_scatter | solution.py:225
  747.7 22.5 %copy-start.19 = (bf16[1280,4,32]{0,2,1:T(8,128)(2,1)S(1)}, bf16[1280,4,32]{0,2,1:T(8,128)(2,1)}, u32[]{:S(2)}) copy-start(bf16[1280,4,32]{0,2,1:T(8,128)(2,1)} %copy-done.18) | copy-start | bytes 983044
  747.7 22.4 %copy-start.21 = (bf16[1280,4,32]{0,2,1:T(8,128)(2,1)S(1)}, bf16[1280,4,32]{0,2,1:T(8,128)(2,1)}, u32[]{:S(2)}) copy-start(bf16[1280,4,32]{0,2,1:T(8,128)(2,1)} %copy-done.20) | copy-start | bytes 983044
  770.2 9.0 copy-start.15
  770.2 9.0 copy-start.17
  770.2 16.7 %slice-start = ((s8[5242880]{0:T(1024)(128)(4,1)}), s8[1048576]{0:T(1024)(128)(4,1)S(1)}, s32[]{:S(2)}) async-start(s8[5242880]{0:T(1024)(128)(4,1)} %bitcast.102), calls=%async_computation.32 | async-start | bytes 2097152
  779.2 7.3 copy-start.11
  779.2 7.3 copy-start.27
  779.2 7.7 slice-start.1
  789.6 268.3 %reduce-scatter.20.cloned.1.call-start = ((), (), s32[]{:S(2)}) async-start(), calls=%async_computation.25 | async-start | bytes 1310720 | tf_op jit(solution)/shard_map/reduce_scatter | solution.py:222
  794.8 322.0 %reduce-scatter.18.cloned.1.call-start = ((), (), s32[]{:S(2)}) async-start(), calls=%async_computation.24 | async-start | bytes 5898240 | tf_op jit(solution)/shard_map/reduce_scatter | solution.py:215
  795.1 2.9 copy-start.22
  798.0 5.6 copy-start.24
  812.0 365.3 %reduce-scatter.14.cloned.1.call-start = ((), (), s32[]{:S(2)}) async-start(), calls=%async_computation.21 | async-start | bytes 5898240 | tf_op jit(solution)/shard_map/reduce_scatter | solution.py:164
  824.9 291.8 %copy-start.1 = (bf16[160,2048]{1,0:T(8,128)(2,1)S(1)}, bf16[160,2048]{1,0:T(8,128)(2,1)}, u32[]{:S(2)}) copy-start(bf16[160,2048]{1,0:T(8,128)(2,1)} %param.12) | copy-start | bytes 1966084
  824.9 291.8 %copy-start.29 = (f32[2048]{0:T(1024)S(1)}, f32[2048]{0:T(1024)}, u32[]{:S(2)}) copy-start(f32[2048]{0:T(1024)} %copy-done.28) | copy-start | bytes 24580
  824.9 291.8 %copy-start.31 = (f32[160]{0:T(256)S(1)}, f32[160]{0:T(256)}, u32[]{:S(2)}) copy-start(f32[160]{0:T(256)} %copy-done.30) | copy-start | bytes 1924
  824.9 352.4 %copy-start.2 = (f32[160,2048]{1,0:T(8,128)S(1)}, f32[160,2048]{1,0:T(8,128)}, u32[]{:S(2)}) copy-start(f32[160,2048]{1,0:T(8,128)} %reduce-scatter.16.cloned.1.call-done) | copy-start | bytes 3932164
  (3 other events, 2.2 us)
Sparse Core Ops, SparseCore 0:
  9.6 30.6 all-gather.16
  42.8 40.5 all-gather.10
  84.9 27.9 all-gather.14
  114.3 27.4 all-gather.12
  143.2 27.4 all-gather.18
  177.5 81.0 reduce-scatter.11
  260.1 80.7 all-gather.24
  343.4 39.6 all-gather.20
  384.6 80.7 all-gather.22
  466.8 79.2 all-gather.26
  580.0 80.0 reduce-scatter.15
  664.6 41.0 all-gather.28
  708.0 76.7 reduce-scatter.31
  787.0 77.2 reduce-scatter.29
  866.5 77.2 reduce-scatter.27
  946.0 27.6 reduce-scatter.25
  975.8 25.7 reduce-scatter.23
  1003.9 25.7 reduce-scatter.21
  1032.0 25.7 reduce-scatter.19
  1061.5 55.2 reduce-scatter.17
  1120.1 57.1 reduce-scatter.13
